TPU v7x, 32 devices: a whole 2x2x4 slice. The times are simulated.
32 devices in a mesh: groups: 2 (over x), lon: 8 (over z, y), lat: 2 (over core).
Axes of the slice: x: 2, y: 2, z: 4, core: 2. Of those that a mesh axis runs over, the one named last changes fastest.
Arguments:
- atmosphere: bfloat16 [256, 128, 512], P(('groups', 'lat'), 'lon'), parts along dimension 0, may hold values from -6 to 6
- pole_band: int32 [256], P(('groups', 'lat')), parts along dimension 0, may hold values from 0 to 15, never falling along the last dimension, each value on 1 to 96 neighbouring positions
- key_valid: int32 [256, 128], P(('groups', 'lat'), 'lon'), parts along dimension 0, may hold values 0 or 1
- norm_gains: float32 [2, 2, 512], replicated, may hold values from 0.5 to 1.5
- attend_in: bfloat16 [2, 512, 1536], replicated, as said below
- attend_out: bfloat16 [2, 512, 512], replicated, may hold values from -0.25 to 0.25
- expand: bfloat16 [2, 512, 1024], replicated, may hold values from -0.25 to 0.25
- contract: bfloat16 [2, 1024, 512], replicated, may hold values from -0.1875 to 0.1875
Outputs:
- evolved: bfloat16 [256, 128, 512], P(('groups', 'lat'), 'lon'), parts along dimension 0
There are 2 independent parts, one for each index of `groups`. A program takes and returns all parts, laid end to end along the dimension named above; an argument that names none is the same for every part. Nothing has to cross between parts.
Inputs may be any that keep to these rules, and one draw needn't show every extreme that they name: `pole_band`: band numbers never fall along latitude, every number from 0 to the largest is used, and a band holds 1 to 96 rows. `attend_in`: query and value entries of order one over the square root of 512.
All inputs are finite; a program needn't handle non-finite values. No bound on the sum of `key_valid` on one device may be relied on, other than what follows from the above.
Results may differ from a plain program's by a relative error of at most 0.011.
Values may be sent and summed in bfloat16 or wider, within the bound.
A program may use at most 128 MiB of HBM per device.

v0:
```python
import functools
import math

import jax
import jax.numpy as jnp
from jax import lax
from jax.experimental import pallas as pl
from jax.experimental.pallas import tpu as pltpu
from jax.sharding import PartitionSpec as P

H = 8
WH = 32
SH = 16
SW = 8
EPS = 1e-05
MESH = pl.DeviceIdType.MESH
F32 = jnp.float32
BF16 = jnp.bfloat16


def norm(wide, gains):
    centred = wide - jnp.mean(wide, -1, keepdims=True)
    spread = jnp.mean(centred * centred, -1, keepdims=True)
    return (centred * lax.rsqrt(spread + EPS) * gains).astype(BF16)


def gelu(v):
    inner = v * (math.sqrt(2.0 / math.pi) + (math.sqrt(2.0 / math.pi) * 0.044715) * (v * v))
    half = 0.5 * v
    return half + half * jnp.tanh(inner)


def kernel(
    names, sizes, atm, band, valid, gains, w_in, w_out, w_up, w_down, out,
    xs, ys, code, cs, win, wout, wup, wdown, q2, ks, vs, bias, ctx, send, recv, local,
):
    height = atm.shape[0]
    width = atm.shape[2]
    count = height // WH
    cells = WH * SW
    pairs = width // 128
    body = height - SH
    last = height // SH - 1
    at = {name: lax.axis_index(name) for name in names}

    def device(lat, lon):
        spot = dict(at)
        spot["lat"] = lax.rem(at["lat"] + lat + sizes["lat"], sizes["lat"])
        spot["lon"] = lax.rem(at["lon"] + lon + sizes["lon"], sizes["lon"])
        return tuple(spot[name] for name in names)

    loads = []

    def load(src, dst):
        copy = pltpu.make_async_copy(src, dst, local.at[len(loads)])
        copy.start()
        loads.append(copy)
        return copy

    own = load(atm.at[pl.ds(SH, body), pl.ds(SW, SW), :], xs.at[0, 0, pl.ds(0, body)])
    weights = {}
    for layer in range(2):
        for name, src, dst in (
            ("in", w_in, win), ("out", w_out, wout), ("up", w_up, wup), ("down", w_down, wdown),
        ):
            weights[name, layer] = load(src.at[layer], dst.at[layer])

    mixed = (2 * band[...] + valid[...]).astype(F32).astype(BF16)
    lane = lax.broadcasted_iota(jnp.int32, (mixed.shape[0], SH * SW), 1)
    column = lax.broadcasted_iota(jnp.int32, (mixed.shape[0], SH * SW), 0)
    lane_row = lax.broadcasted_iota(jnp.int32, (SH, SH * SW), 1) // SW
    keep = lane_row == lax.broadcasted_iota(jnp.int32, (SH, SH * SW), 0)
    for h in range(2):
        pick = jnp.where(column == lane % SW + SW * h, 1.0, 0.0).astype(BF16)
        spread = lax.dot_general(
            mixed, pick, (((0,), (0,)), ((), ())), preferred_element_type=F32)
        for chunk in range(last + 1):
            rows = jnp.where(keep, spread[SH * chunk:SH * chunk + SH], 0.0)
            rows = jnp.sum(rows, 0, keepdims=True).astype(jnp.int32)
            code[h, chunk] = jnp.broadcast_to(rows, (8, SH * SW))

    barrier = pltpu.get_barrier_semaphore()
    around = ((-1, 0), (0, -1), (-1, -1), (1, 0), (0, 1), (1, 1))
    for lat, lon in around:
        pl.semaphore_signal(barrier, inc=1, device_id=device(lat, lon), device_id_type=MESH)
    pl.semaphore_wait(barrier, len(around))

    sent = []

    def push(src, dst, lat, lon):
        copy = pltpu.make_async_remote_copy(
            src_ref=src, dst_ref=dst, send_sem=send.at[len(sent)], recv_sem=recv.at[len(sent)],
            device_id=device(lat, lon), device_id_type=MESH,
        )
        copy.start()
        sent.append(copy)
        return copy

    west, east = pl.ds(0, SW), pl.ds(SW, SW)
    got = [[] for _ in range(count)]
    got_code = []
    for w in range(count):
        rows = WH if w < count - 1 else WH - SH
        got[w].append(push(
            atm.at[pl.ds(SH + w * WH, rows), west, :], xs.at[0, 1, pl.ds(w * WH, rows)], 0, -1))
        if w == 0:
            got_code.append(push(code.at[0, pl.ds(1, last)], cs.at[1, pl.ds(0, last)], 0, -1))
            got_code.append(push(code.at[1, pl.ds(0, 1)], cs.at[0, pl.ds(last, 1)], -1, 0))
            got_code.append(push(code.at[0, pl.ds(0, 1)], cs.at[1, pl.ds(last, 1)], -1, -1))
            got_lat = push(atm.at[pl.ds(0, SH), east, :], xs.at[0, 0, pl.ds(body, SH)], -1, 0)
    got[count - 1].append(push(
        atm.at[pl.ds(0, SH), west, :], xs.at[0, 1, pl.ds(body, SH)], -1, -1))

    vs[:, :, pl.ds(64, 16), :] = jnp.ones(vs.shape[:2] + (16, vs.shape[3]), BF16)
    low = lax.broadcasted_iota(jnp.int32, (cells, 128), 1) < 64
    scale = math.log2(math.e) / math.sqrt(64)

    def codes_of(layer, w):
        found = []
        for h in range(2):
            for chunk in (2 * w, 2 * w + 1):
                if layer == 1:
                    found.append(code[1 - h, chunk])
                elif h == 0 and chunk < last:
                    found.append(code[1, chunk + 1])
                else:
                    found.append(cs[h, chunk])
        return found

    def make_bias(layer, w):
        found = codes_of(layer, w)
        across = jnp.concatenate(found, 1)[0:1]
        total = across.shape[1]
        band_across = jnp.broadcast_to(across >> 1, (128, total))
        row = lax.broadcasted_iota(jnp.int32, (128, total), 0)
        col = lax.broadcasted_iota(jnp.int32, (128, total), 1)
        for i, one in enumerate(found):
            down = jnp.broadcast_to(one[0:1].astype(F32), (128, 128)).T.astype(jnp.int32)
            down = jnp.concatenate([down] * (total // 128), 1)
            allowed = ((down >> 1) == band_across) & (((down & 1) == 1) | (row + 128 * i == col))
            bias[w, pl.ds(128 * i, 128), :] = jnp.where(allowed, 0.0, -1e30)

    def field(layer, w, h):
        return xs[layer, h, pl.ds(w * WH, WH)].astype(F32).reshape(cells, width)

    def project(layer, w, h):
        normed = norm(field(layer, w, h), gains[layer, 0:1, :])
        rows = pl.ds(h * cells, cells)
        for part in range(3):
            made = jnp.dot(
                normed, win[layer, :, pl.ds(part * width, width)], preferred_element_type=F32)
            if part == 2:
                turned = made.T.astype(BF16)
                for head in range(2 * pairs):
                    vs[w, head, pl.ds(0, 64), rows] = turned[64 * head:64 * head + 64]
                continue
            for p in range(pairs):
                two = made[:, 128 * p:128 * p + 128]
                if part == 0:
                    two = two * scale
                    q2[w, p, h, pl.ds(0, cells), :] = jnp.where(low, two, 0.0).astype(BF16)
                    q2[w, p, h, pl.ds(cells, cells), :] = jnp.where(low, 0.0, two).astype(BF16)
                else:
                    ks[w, p, rows, :] = two.astype(BF16)

    half_keys = cells

    def attend(layer, w, h, slot):
        heads = 2 * pairs
        scores = [[None, None] for _ in range(heads)]
        tops = [[None, None] for _ in range(heads)]

        def score(j, c):
            p, odd = j // 2, j % 2
            rows = pl.ds(half_keys * c, half_keys)
            made = lax.dot_general(
                ks[w, p, rows, :], q2[w, p, h, pl.ds(cells * odd, cells), :],
                (((1,), (1,)), ((), ())), preferred_element_type=F32)
            made = made + bias[w, rows, pl.ds(h * cells, cells)]
            scores[j][c] = made
            tops[j][c] = jnp.max(made, 0, keepdims=True)

        def weigh(j, c, top):
            raw = jnp.exp2(scores[j][c] - top).astype(BF16)
            scores[j][c] = None
            return jnp.dot(
                vs[w, j, :, pl.ds(half_keys * c, half_keys)], raw, preferred_element_type=F32)

        for j in range(heads + 1):
            made = None
            top = None if j == 0 else jnp.maximum(tops[j - 1][0], tops[j - 1][1])
            for c in range(2):
                if j < heads:
                    score(j, c)
                if j > 0:
                    part = weigh(j - 1, c, top)
                    made = part if made is None else made + part
            if j > 0:
                ctx[slot, pl.ds(64 * (j - 1), 64), :] = made[:64] / made[64:65]
            yield

    def finish(layer, w, h, slot, done):
        step = 256
        turned = ctx[slot].T.astype(BF16)
        own_field = field(layer, w, h)
        parts = []
        for n in range(0, width, step):
            parts.append(own_field[:, n:n + step] + jnp.dot(
                turned, wout[layer, :, pl.ds(n, step)], preferred_element_type=F32))
            yield
        resid = jnp.concatenate(parts, 1).astype(BF16).astype(F32)
        normed = norm(resid, gains[layer, 1:2, :])
        yield
        hidden = []
        for n in range(0, wup.shape[2], step):
            hidden.append(gelu(jnp.dot(
                normed, wup[layer, :, pl.ds(n, step)], preferred_element_type=F32)).astype(BF16))
            yield
        hidden = jnp.concatenate(hidden, 1)
        parts = []
        for n in range(0, width, step):
            parts.append(resid[:, n:n + step] + jnp.dot(
                hidden, wdown[layer, :, pl.ds(n, step)], preferred_element_type=F32))
            yield
        done(jnp.concatenate(parts, 1).reshape(WH, SW, width).astype(BF16))

    def together(*works):
        works = list(works)
        while works:
            for work in list(works):
                if next(work, works) is works:
                    works.remove(work)

    own.wait()
    weights["in", 0].wait()
    for w in range(count):
        if w == count - 1:
            got_lat.wait_recv()
        project(0, w, 0)
    for copy in got_code:
        copy.wait_recv()
    for w in range(count):
        make_bias(0, w)
    back = {}

    def send_east(w):
        rows = WH if w < count - 1 else WH - SH

        def done(made):
            ys[0, 1, pl.ds(w * WH, WH)] = made
            back[w] = push(
                ys.at[0, 1, pl.ds(w * WH, rows)], xs.at[1, 1, pl.ds(SH + w * WH, rows)], 0, 1)
            if w == count - 1:
                back["corner"] = push(
                    ys.at[0, 1, pl.ds(body, SH)], xs.at[1, 1, pl.ds(0, SH)], 1, 1)

        return done

    def keep_own(w):
        rows = WH if w < count - 1 else WH - SH

        def done(made):
            xs[1, 0, pl.ds(SH + w * WH, rows)] = made[:rows]
            if w == count - 1:
                ys[0, 0, pl.ds(body, SH)] = made[rows:]
                back["lat"] = push(
                    ys.at[0, 0, pl.ds(body, SH)], xs.at[1, 0, pl.ds(0, SH)], 1, 0)

        return done

    def give(w, h):
        def done(made):
            out[pl.ds(w * WH, WH), pl.ds(SW * (1 - h), SW), :] = made

        return done

    waiting = None
    for w in range(count):
        for copy in got[w]:
            copy.wait_recv()
        project(0, w, 1)
        together(attend(0, w, 1, 0), *([waiting] if waiting else []))
        if w == 0:
            for name in ("out", "up", "down"):
                weights[name, 0].wait()
        together(attend(0, w, 0, 1), finish(0, w, 1, 0, send_east(w)))
        waiting = finish(0, w, 0, 1, keep_own(w))
    weights["in", 1].wait()
    for w in range(count):
        make_bias(1, w)
    together(waiting)

    for name in ("out", "up", "down"):
        weights[name, 1].wait()
    for w in reversed(range(count)):
        if w == 0:
            back["lat"].wait_recv()
        project(1, w, 0)
    waiting = None
    waited = set()
    for w in reversed(range(count)):
        for v in (w - 1, w):
            if v >= 0 and v not in waited:
                waited.add(v)
                back[v].wait_recv()
        if w == 0:
            back["corner"].wait_recv()
        project(1, w, 1)
        together(attend(1, w, 0, 0), *([waiting] if waiting else []))
        together(attend(1, w, 1, 1), finish(1, w, 0, 0, give(w, 0)))
        waiting = finish(1, w, 1, 1, give(w, 1))
    together(waiting)
    for copy in sent:
        copy.wait_send()


def solution(mesh):
    names = tuple(mesh.axis_names)
    sizes = dict(mesh.shape)

    def on_device(atm, band, valid, gains, w_in, w_out, w_up, w_down):
        height, breadth, width = atm.shape
        hidden = w_up.shape[2]
        count = height // WH
        cells = WH * SW
        pairs = width // 128
        chunks = height // SH
        anyspace = pl.BlockSpec(memory_space=pl.ANY)
        vmem = pl.BlockSpec(memory_space=pltpu.VMEM)
        pushes = 2 * count + 7
        return pl.pallas_call(
            functools.partial(kernel, names, sizes),
            out_shape=pltpu.VMEM(atm.shape, BF16),
            in_specs=[anyspace, vmem, vmem, vmem] + [anyspace] * 4,
            out_specs=vmem,
            scratch_shapes=[
                pltpu.VMEM((2, 2, height, SW, width), BF16),
                pltpu.VMEM((1, 2, height, SW, width), BF16),
                pltpu.VMEM((2, chunks, 8, SH * SW), jnp.int32),
                pltpu.VMEM((2, chunks, 8, SH * SW), jnp.int32),
                pltpu.VMEM(w_in.shape, BF16),
                pltpu.VMEM(w_out.shape, BF16),
                pltpu.VMEM(w_up.shape, BF16),
                pltpu.VMEM(w_down.shape, BF16),
                pltpu.VMEM((count, pairs, 2, 2 * cells, 128), BF16),
                pltpu.VMEM((count, pairs, 2 * cells, 128), BF16),
                pltpu.VMEM((count, 2 * pairs, 80, 2 * cells), BF16),
                pltpu.VMEM((count, 2 * cells, 2 * cells), F32),
                pltpu.VMEM((2, width, cells), F32),
                pltpu.SemaphoreType.DMA((pushes,)),
                pltpu.SemaphoreType.DMA((pushes,)),
                pltpu.SemaphoreType.DMA((9,)),
            ],
            compiler_params=pltpu.CompilerParams(
                collective_id=0, has_side_effects=True, vmem_limit_bytes=56 * 1024 * 1024
            ),
        )(atm, band[None, :], valid.T, gains, w_in, w_out, w_up, w_down)

    rows = P(("groups", "lat"), "lon", None)
    return jax.shard_map(
        on_device,
        mesh=mesh,
        in_specs=(rows, P(("groups", "lat")), P(("groups", "lat"), "lon"), P(), P(), P(), P(), P()),
        out_specs=rows,
        check_vma=False,
    )
```

profile of v0, /device:TPU:0, one launch (start us, length us, event | category | flops | bytes accessed | tf_op | source)
XLA Modules:
  0.0 46.9 jit_solution(16516234228267197002)
XLA Ops:
  0.0 45.9 %shard_map.82 = bf16[64,16,512]{2,1,0:T(8,128)(2,1)S(1)} custom-call(bf16[64,16,512]{2,1,0:T(8,128)(2,1)} %atm.1, s32[1,64]{1,0:T(1,128)} %bitcast.3, s32[16,64]{1,0:T(8,128)} %bitcast.2, f32[2,2,512]{2,1,0:T(2,128)} %gains.1, bf16[2,512,1536]{2,1,0:T(8,128)(2,1)} %w_in.1, bf16[2,512,512]{2,1,0:T(8,128)(2,1)} %w_out.1, bf16[2,512,1024]{2,1,0:T(8,128)(2,1)} %w_up.1, ...), custom_call_target="tpu_custom_call" | custom-call | tf_op jit(solution)/shard_map/pallas_call | solution.py:331
  45.9 1.0 %copy.10 = bf16[64,16,512]{2,1,0:T(8,128)(2,1)} copy(bf16[64,16,512]{2,1,0:T(8,128)(2,1)S(1)} %shard_map.82) | data formatting | bytes 2097152
where the time goes:
time: 47.2 us; the launch traced here: 46.9 us
  Pallas kernels  45.9 us (97%)
  local copies, waits for them, and re-layouts  0.97 us (2%)
    pallas_call x1, Pallas kernels, on_device(): pl.pallas_call(functools.partial(kernel, names, sizes), out_shape=pltpu.V...  45.9 us
    unnamed x1, local copies, waits for them, and re-layouts  0.97 us

commit v1 on v0

--- a/solution.py
+++ b/solution.py
@@ -31,8 +31,9 @@
 
 
 def kernel(
-    names, sizes, atm, band, valid, gains, w_in, w_out, w_up, w_down, out,
-    xs, ys, code, cs, win, wout, wup, wdown, q2, ks, vs, bias, ctx, send, recv, local,
+    names, sizes, atm, band_in, valid_in, gains_in, w_in, w_out, w_up, w_down, out,
+    xs, ys, code, cs, band, valid, gains, win, wout, wup, wdown, q2, ks, vs, bias, ctx,
+    send, recv, local,
 ):
     height = atm.shape[0]
     width = atm.shape[2]
@@ -49,6 +50,11 @@
         spot["lon"] = lax.rem(at["lon"] + lon + sizes["lon"], sizes["lon"])
         return tuple(spot[name] for name in names)
 
+    barrier = pltpu.get_barrier_semaphore()
+    sources = ((1, 0), (0, -1), (1, -1))
+    for lat, lon in sources:
+        pl.semaphore_signal(barrier, inc=1, device_id=device(lat, lon), device_id_type=MESH)
+
     loads = []
 
     def load(src, dst):
@@ -57,7 +63,9 @@
         loads.append(copy)
         return copy
 
-    own = load(atm.at[pl.ds(SH, body), pl.ds(SW, SW), :], xs.at[0, 0, pl.ds(0, body)])
+    west, east = pl.ds(0, SW), pl.ds(SW, SW)
+    small = [load(band_in, band), load(valid_in, valid), load(gains_in, gains)]
+    own = load(atm.at[pl.ds(SH, body), west, :], xs.at[0, 0, pl.ds(0, body)])
     weights = {}
     for layer in range(2):
         for name, src, dst in (
@@ -65,6 +73,8 @@
         ):
             weights[name, layer] = load(src.at[layer], dst.at[layer])
 
+    for copy in small:
+        copy.wait()
     mixed = (2 * band[...] + valid[...]).astype(F32).astype(BF16)
     lane = lax.broadcasted_iota(jnp.int32, (mixed.shape[0], SH * SW), 1)
     column = lax.broadcasted_iota(jnp.int32, (mixed.shape[0], SH * SW), 0)
@@ -79,11 +89,7 @@
             rows = jnp.sum(rows, 0, keepdims=True).astype(jnp.int32)
             code[h, chunk] = jnp.broadcast_to(rows, (8, SH * SW))
 
-    barrier = pltpu.get_barrier_semaphore()
-    around = ((-1, 0), (0, -1), (-1, -1), (1, 0), (0, 1), (1, 1))
-    for lat, lon in around:
-        pl.semaphore_signal(barrier, inc=1, device_id=device(lat, lon), device_id_type=MESH)
-    pl.semaphore_wait(barrier, len(around))
+    pl.semaphore_wait(barrier, len(sources))
 
     sent = []
 
@@ -96,20 +102,17 @@
         sent.append(copy)
         return copy
 
-    west, east = pl.ds(0, SW), pl.ds(SW, SW)
-    got = [[] for _ in range(count)]
-    got_code = []
+    got_code = [
+        push(code.at[1, pl.ds(1, last)], cs.at[1, pl.ds(0, last)], 0, 1),
+        push(code.at[0, pl.ds(0, 1)], cs.at[0, pl.ds(last, 1)], -1, 0),
+        push(code.at[1, pl.ds(0, 1)], cs.at[1, pl.ds(last, 1)], -1, 1),
+    ]
+    got = []
     for w in range(count):
         rows = WH if w < count - 1 else WH - SH
-        got[w].append(push(
-            atm.at[pl.ds(SH + w * WH, rows), west, :], xs.at[0, 1, pl.ds(w * WH, rows)], 0, -1))
-        if w == 0:
-            got_code.append(push(code.at[0, pl.ds(1, last)], cs.at[1, pl.ds(0, last)], 0, -1))
-            got_code.append(push(code.at[1, pl.ds(0, 1)], cs.at[0, pl.ds(last, 1)], -1, 0))
-            got_code.append(push(code.at[0, pl.ds(0, 1)], cs.at[1, pl.ds(last, 1)], -1, -1))
-            got_lat = push(atm.at[pl.ds(0, SH), east, :], xs.at[0, 0, pl.ds(body, SH)], -1, 0)
-    got[count - 1].append(push(
-        atm.at[pl.ds(0, SH), west, :], xs.at[0, 1, pl.ds(body, SH)], -1, -1))
+        got.append([push(
+            atm.at[pl.ds(SH + w * WH, rows), east, :], xs.at[0, 1, pl.ds(w * WH, rows)], 0, 1)])
+    got_lat = push(atm.at[pl.ds(0, SH), west, :], xs.at[0, 0, pl.ds(body, SH)], -1, 0)
 
     vs[:, :, pl.ds(64, 16), :] = jnp.ones(vs.shape[:2] + (16, vs.shape[3]), BF16)
     low = lax.broadcasted_iota(jnp.int32, (cells, 128), 1) < 64
@@ -120,9 +123,9 @@
         for h in range(2):
             for chunk in (2 * w, 2 * w + 1):
                 if layer == 1:
-                    found.append(code[1 - h, chunk])
+                    found.append(code[h, chunk])
                 elif h == 0 and chunk < last:
-                    found.append(code[1, chunk + 1])
+                    found.append(code[0, chunk + 1])
                 else:
                     found.append(cs[h, chunk])
         return found
@@ -241,20 +244,24 @@
         copy.wait_recv()
     for w in range(count):
         make_bias(0, w)
+    got[0][0].wait_send()
+    got[count - 1].append(push(
+        atm.at[pl.ds(0, SH), east, :], xs.at[0, 1, pl.ds(body, SH)], -1, 1))
     back = {}
 
-    def send_east(w):
+    def send_west(w):
         rows = WH if w < count - 1 else WH - SH
 
         def done(made):
             ys[0, 1, pl.ds(w * WH, WH)] = made
             back[w] = push(
-                ys.at[0, 1, pl.ds(w * WH, rows)], xs.at[1, 1, pl.ds(SH + w * WH, rows)], 0, 1)
-            if w == count - 1:
-                back["corner"] = push(
-                    ys.at[0, 1, pl.ds(body, SH)], xs.at[1, 1, pl.ds(0, SH)], 1, 1)
+                ys.at[0, 1, pl.ds(w * WH, rows)], xs.at[1, 1, pl.ds(SH + w * WH, rows)], 0, -1)
 
         return done
+
+    def send_corner():
+        back["corner"] = push(
+            ys.at[0, 1, pl.ds(body, SH)], xs.at[1, 1, pl.ds(0, SH)], 1, -1)
 
     def keep_own(w):
         rows = WH if w < count - 1 else WH - SH
@@ -270,7 +277,7 @@
 
     def give(w, h):
         def done(made):
-            out[pl.ds(w * WH, WH), pl.ds(SW * (1 - h), SW), :] = made
+            out[pl.ds(w * WH, WH), pl.ds(SW * h, SW), :] = made
 
         return done
 
@@ -283,7 +290,7 @@
         if w == 0:
             for name in ("out", "up", "down"):
                 weights[name, 0].wait()
-        together(attend(0, w, 0, 1), finish(0, w, 1, 0, send_east(w)))
+        together(attend(0, w, 0, 1), finish(0, w, 1, 0, send_west(w)))
         waiting = finish(0, w, 0, 1, keep_own(w))
     weights["in", 1].wait()
     for w in range(count):
@@ -296,6 +303,8 @@
         if w == 0:
             back["lat"].wait_recv()
         project(1, w, 0)
+        if w == count - 1:
+            send_corner()
     waiting = None
     waited = set()
     for w in reversed(range(count)):
@@ -311,7 +320,8 @@
         waiting = finish(1, w, 1, 1, give(w, 1))
     together(waiting)
     for copy in sent:
-        copy.wait_send()
+        if copy is not got[0][0]:
+            copy.wait_send()
 
 
 def solution(mesh):
@@ -331,13 +341,16 @@
         return pl.pallas_call(
             functools.partial(kernel, names, sizes),
             out_shape=pltpu.VMEM(atm.shape, BF16),
-            in_specs=[anyspace, vmem, vmem, vmem] + [anyspace] * 4,
+            in_specs=[anyspace] * 8,
             out_specs=vmem,
             scratch_shapes=[
                 pltpu.VMEM((2, 2, height, SW, width), BF16),
                 pltpu.VMEM((1, 2, height, SW, width), BF16),
                 pltpu.VMEM((2, chunks, 8, SH * SW), jnp.int32),
                 pltpu.VMEM((2, chunks, 8, SH * SW), jnp.int32),
+                pltpu.VMEM((1, height), jnp.int32),
+                pltpu.VMEM((breadth, height), jnp.int32),
+                pltpu.VMEM(gains.shape, F32),
                 pltpu.VMEM(w_in.shape, BF16),
                 pltpu.VMEM(w_out.shape, BF16),
                 pltpu.VMEM(w_up.shape, BF16),
@@ -349,7 +362,7 @@
                 pltpu.VMEM((2, width, cells), F32),
                 pltpu.SemaphoreType.DMA((pushes,)),
                 pltpu.SemaphoreType.DMA((pushes,)),
-                pltpu.SemaphoreType.DMA((9,)),
+                pltpu.SemaphoreType.DMA((12,)),
             ],
             compiler_params=pltpu.CompilerParams(
                 collective_id=0, has_side_effects=True, vmem_limit_bytes=56 * 1024 * 1024

time: 47.2 us -> 40.6 us (0.86)
  Pallas kernels: 45.9 us -> 39.5 us
    pallas_call x1, Pallas kernels: 45.9 us -> 39.5 us  [on_device(): pl.pallas_call(functools.partial(kernel, names, sizes), out_shape=pltpu.V...]
where the time goes in v1:
time: 40.6 us; the launch traced here: 40.5 us
  Pallas kernels  39.5 us (97%)
  local copies, waits for them, and re-layouts  0.97 us (2%)
    pallas_call x1, Pallas kernels, on_device(): pl.pallas_call(functools.partial(kernel, names, sizes), out_shape=pltpu.V...  39.5 us
    unnamed x1, local copies, waits for them, and re-layouts  0.97 us

profile of v1, /device:TPU:0, one launch (start us, length us, event | category | flops | bytes accessed | tf_op | source)
XLA Modules:
  0.0 40.5 jit_solution(17726165114966775131)
XLA Ops:
  0.0 39.5 %shard_map.82 = bf16[64,16,512]{2,1,0:T(8,128)(2,1)S(1)} custom-call(bf16[64,16,512]{2,1,0:T(8,128)(2,1)} %atm.1, s32[1,64]{1,0:T(1,128)} %bitcast.3, s32[16,64]{1,0:T(8,128)} %bitcast.2, f32[2,2,512]{2,1,0:T(2,128)} %gains_in.1, bf16[2,512,1536]{2,1,0:T(8,128)(2,1)} %w_in.1, bf16[2,512,512]{2,1,0:T(8,128)(2,1)} %w_out.1, bf16[2,512,1024]{2,1,0:T(8,128)(2,1)} %w_up.1, ...), custom_call_target="tpu_custom_call" | custom-call | tf_op jit(solution)/shard_map/pallas_call | solution.py:341
  39.5 1.0 %copy.10 = bf16[64,16,512]{2,1,0:T(8,128)(2,1)} copy(bf16[64,16,512]{2,1,0:T(8,128)(2,1)S(1)} %shard_map.82) | data formatting | bytes 2097152

commit v2 on v1

v2 whole, which is shorter than its diff:
```python
import functools
import math

import jax
import jax.numpy as jnp
from jax import lax
from jax.experimental import pallas as pl
from jax.experimental.pallas import tpu as pltpu
from jax.sharding import PartitionSpec as P

H = 8
WH = 32
SH = 16
SW = 8
EPS = 1e-05
MESH = pl.DeviceIdType.MESH
F32 = jnp.float32
BF16 = jnp.bfloat16
BAND_BITS = 7
FAR = -1e30
DEPTH = 3


def norm(wide, gains):
    centred = wide - jnp.mean(wide, -1, keepdims=True)
    spread = jnp.mean(centred * centred, -1, keepdims=True)
    return (centred * lax.rsqrt(spread + EPS) * gains).astype(BF16)


def gelu_of_twice(u):
    root = math.sqrt(2.0 / math.pi)
    inner = u * (2.0 * root + (8.0 * root * 0.044715) * (u * u))
    return u + u * jnp.tanh(inner)


def kernel(
    names, sizes, atm, band_in, valid_in, gains_in, w_in, w_out, w_up, w_down, out,
    xs, ys, code, cs, band, valid, gains, win, wout, wup, wdown, q2, ks, vs, mask, acc, ctx,
    send, recv, local,
):
    height = atm.shape[0]
    width = atm.shape[2]
    count = height // WH
    cells = WH * SW
    pairs = width // 128
    body = height - SH
    last = height // SH - 1
    at = {name: lax.axis_index(name) for name in names}

    def device(lat, lon):
        spot = dict(at)
        spot["lat"] = lax.rem(at["lat"] + lat + sizes["lat"], sizes["lat"])
        spot["lon"] = lax.rem(at["lon"] + lon + sizes["lon"], sizes["lon"])
        return tuple(spot[name] for name in names)

    barrier = pltpu.get_barrier_semaphore()
    sources = ((1, 0), (0, -1), (1, -1))
    for lat, lon in sources:
        pl.semaphore_signal(barrier, inc=1, device_id=device(lat, lon), device_id_type=MESH)

    loads = []

    def load(src, dst):
        copy = pltpu.make_async_copy(src, dst, local.at[len(loads)])
        copy.start()
        loads.append(copy)
        return copy

    west, east = pl.ds(0, SW), pl.ds(SW, SW)
    small = [load(band_in, band), load(valid_in, valid), load(gains_in, gains)]
    own = load(atm.at[pl.ds(SH, body), west, :], xs.at[0, 0, pl.ds(0, body)])
    weights = {}
    for layer in range(2):
        for name, src, dst in (
            ("in", w_in, win), ("out", w_out, wout), ("up", w_up, wup), ("down", w_down, wdown),
        ):
            weights[name, layer] = load(src.at[layer], dst.at[layer])

    for copy in small:
        copy.wait()
    mixed = (2 * band[...] + valid[...]).astype(F32).astype(BF16)
    lane = lax.broadcasted_iota(jnp.int32, (mixed.shape[0], SH * SW), 1)
    column = lax.broadcasted_iota(jnp.int32, (mixed.shape[0], SH * SW), 0)
    lane_row = lax.broadcasted_iota(jnp.int32, (SH, SH * SW), 1) // SW
    keep = lane_row == lax.broadcasted_iota(jnp.int32, (SH, SH * SW), 0)
    for h in range(2):
        pick = jnp.where(column == lane % SW + SW * h, 1.0, 0.0).astype(BF16)
        spread = lax.dot_general(
            mixed, pick, (((0,), (0,)), ((), ())), preferred_element_type=F32)
        for chunk in range(last + 1):
            rows = jnp.where(keep, spread[SH * chunk:SH * chunk + SH], 0.0)
            rows = jnp.sum(rows, 0, keepdims=True).astype(jnp.int32)
            code[h, chunk] = jnp.broadcast_to(rows, (8, SH * SW))

    pl.semaphore_wait(barrier, len(sources))

    sent = []

    def push(src, dst, lat, lon):
        copy = pltpu.make_async_remote_copy(
            src_ref=src, dst_ref=dst, send_sem=send.at[len(sent)], recv_sem=recv.at[len(sent)],
            device_id=device(lat, lon), device_id_type=MESH,
        )
        copy.start()
        sent.append(copy)
        return copy

    got_code = [
        push(code.at[1, pl.ds(1, last)], cs.at[1, pl.ds(0, last)], 0, 1),
        push(code.at[0, pl.ds(0, 1)], cs.at[0, pl.ds(last, 1)], -1, 0),
        push(code.at[1, pl.ds(0, 1)], cs.at[1, pl.ds(last, 1)], -1, 1),
    ]
    got = []
    for w in range(count):
        rows = WH if w < count - 1 else WH - SH
        got.append([push(
            atm.at[pl.ds(SH + w * WH, rows), east, :], xs.at[0, 1, pl.ds(w * WH, rows)], 0, 1)])
    got_lat = push(atm.at[pl.ds(0, SH), west, :], xs.at[0, 0, pl.ds(body, SH)], -1, 0)

    vs[:, :, pl.ds(64, 16), :] = jnp.ones(vs.shape[:2] + (16, vs.shape[3]), BF16)
    low = lax.broadcasted_iota(jnp.int32, (cells, 128), 1) < 64
    scale = math.log2(math.e) / math.sqrt(64)

    def codes_of(layer, w, h):
        found = []
        for chunk in (2 * w, 2 * w + 1):
            if layer == 1:
                found.append(code[h, chunk])
            elif h == 0 and chunk < last:
                found.append(code[0, chunk + 1])
            else:
                found.append(cs[h, chunk])
        return found

    place_bits = (2 * cells - 1).bit_length()
    lanes_used = 2 * (BAND_BITS + place_bits)
    feature = lax.broadcasted_iota(jnp.int32, (128, 128), 1) & 63
    of_band = feature < 2 * BAND_BITS
    used = feature < lanes_used
    pol = feature & 1
    which = jnp.where(of_band, feature // 2 + 1, (feature - 2 * BAND_BITS) // 2)
    weight = jnp.zeros((128, 128), jnp.int32)
    for b in range(max(BAND_BITS + 1, place_bits)):
        weight = jnp.where(which == b, 1 << b, weight)
    weight = jnp.where(used, weight, 0)
    place = lax.broadcasted_iota(jnp.int32, (128, 128), 0)

    def make_mask(layer, w, h):
        for i, one in enumerate(codes_of(layer, w, h)):
            down = jnp.broadcast_to(one[0:1].astype(F32), (128, 128)).T.astype(jnp.int32)
            start = h * cells + 128 * i
            bit = jnp.where((jnp.where(of_band, down, place + start) & weight) != 0, 1, 0)
            match = bit == pol
            counts = used & (of_band | ((down & 1) == 0))
            mask[w, 0, pl.ds(start, 128), :] = jnp.where(match & counts, 1.0, 0.0)
            mask[w, 1, pl.ds(start, 128), :] = jnp.where(match | (feature >= lanes_used), 0.0, FAR)

    def field(layer, w, h, first=0, rows=WH):
        found = xs[layer, h, pl.ds(w * WH + first, rows)]
        return found.astype(F32).reshape(rows * SW, width)

    def project(layer, w, h, first=0, rows=WH):
        def steps():
            normed = norm(field(layer, w, h, first, rows), gains[layer, 0:1, :])
            size = rows * SW
            where = pl.ds(h * cells + first * SW, size)
            yield
            for part in range(3):
                made = jnp.dot(
                    normed, win[layer, :, pl.ds(part * width, width)], preferred_element_type=F32)
                if part == 2:
                    turned = made.T.astype(BF16)
                    for head in range(2 * pairs):
                        vs[w, head, pl.ds(0, 64), where] = turned[64 * head:64 * head + 64]
                    yield
                    continue
                extra = mask[w, 1 - part, where, :]
                for p in range(pairs):
                    two = made[:, 128 * p:128 * p + 128]
                    dst = ks
                    if part == 0:
                        two = two * scale
                        dst = q2
                    dst[w, 2 * p, where, :] = jnp.where(low[:size], two, extra).astype(BF16)
                    dst[w, 2 * p + 1, where, :] = jnp.where(low[:size], extra, two).astype(BF16)
                yield

        return 4, steps()

    heads = 2 * pairs

    def score(w, j, h, c):
        return lax.dot_general(
            ks[w, j, pl.ds(cells * c, cells), :], q2[w, j, pl.ds(cells * h, cells), :],
            (((1,), (1,)), ((), ())), preferred_element_type=F32)

    def weigh(w, j, c, made, top):
        raw = jnp.exp2(made - top).astype(BF16)
        return jnp.dot(
            vs[w, j, :, pl.ds(cells * c, cells)], raw, preferred_element_type=F32)

    def attend(w, h):
        flight = []

        def close():
            j, made, tops = flight.pop(0)
            top = jnp.maximum(tops[0], tops[1])
            total = weigh(w, j, 0, made[0], top) + weigh(w, j, 1, made[1], top)
            ctx[2 * w + h, pl.ds(64 * j, 64), :] = total[:64] / total[64:65]

        def steps():
            for j in range(heads):
                made = [score(w, j, h, c) for c in range(2)]
                flight.append((j, made, [jnp.max(one, 0, keepdims=True) for one in made]))
                if len(flight) > DEPTH:
                    close()
                yield
            while flight:
                close()
                yield

        return heads + DEPTH, steps()

    def attend_half(units, c, close):
        flight = []

        def end():
            w, j, made, top = flight.pop(0)
            close(w, j, weigh(w, j, c, made, top), top)

        def steps():
            for w, j in units:
                made = score(w, j, 0, c)
                flight.append((w, j, made, jnp.max(made, 0, keepdims=True)))
                if len(flight) > 2 * DEPTH:
                    end()
                yield
            while flight:
                end()
                yield

        return len(units) + 2 * DEPTH, steps()

    def attend_own(*windows):
        def close(w, j, part, top):
            acc[w, j, pl.ds(0, 72), :] = part[:72]
            acc[w, j, pl.ds(72, 8), :] = jnp.broadcast_to(top, (8, cells))

        return attend_half([(w, j) for w in windows for j in range(heads)], 0, close)

    def attend_rest(w):
        def close(w, j, part, top):
            first = acc[w, j, pl.ds(0, 64), :]
            first_sum = acc[w, j, pl.ds(64, 8), :][0:1]
            first_top = acc[w, j, pl.ds(72, 8), :][0:1]
            joint = jnp.maximum(first_top, top)
            mine, theirs = jnp.exp2(first_top - joint), jnp.exp2(top - joint)
            share = 1.0 / (first_sum * mine + part[64:65] * theirs)
            ctx[2 * w, pl.ds(64 * j, 64), :] = (
                first * (mine * share) + part[:64] * (theirs * share))

        return attend_half([(w, j) for j in range(heads)], 1, close)

    def finish(layer, w, h, done):
        step = 256

        def steps():
            turned = ctx[2 * w + h].T.astype(BF16)
            own_field = field(layer, w, h)
            parts = []
            for n in range(0, width, step):
                parts.append(own_field[:, n:n + step] + jnp.dot(
                    turned, wout[layer, :, pl.ds(n, step)], preferred_element_type=F32))
                yield
            resid = jnp.concatenate(parts, 1).astype(BF16).astype(F32)
            normed = norm(resid, 0.5 * gains[layer, 1:2, :])
            yield
            hidden = []
            for n in range(0, wup.shape[2], step):
                hidden.append(gelu_of_twice(jnp.dot(
                    normed, wup[layer, :, pl.ds(n, step)], preferred_element_type=F32)).astype(BF16))
                yield
            hidden = jnp.concatenate(hidden, 1)
            parts = []
            for n in range(0, width, step):
                parts.append(resid[:, n:n + step] + jnp.dot(
                    hidden, wdown[layer, :, pl.ds(n, step)], preferred_element_type=F32))
                yield
            done(jnp.concatenate(parts, 1).reshape(WH, SW, width).astype(BF16))

        return 1 + (2 * width + wup.shape[2]) // step, steps()

    def masks(layer):
        def steps():
            for w in range(count):
                for h in range(2):
                    make_mask(layer, w, h)
                    yield

        return 2 * count, steps()

    def chain(*works):
        def steps():
            for _, work in works:
                yield from work

        return sum(size for size, _ in works), steps()

    def together(*works):
        left = [[0, size, work] for size, work in works]
        while left:
            one = min(left, key=lambda it: (it[0] + 1) / it[1])
            one[0] += 1
            if next(one[2], left) is left:
                left.remove(one)

    own.wait()
    weights["in", 0].wait()
    for w in range(count - 1):
        make_mask(0, w, 0)
        together(project(0, w, 0))
    got_code[1].wait_recv()
    make_mask(0, count - 1, 0)
    got_lat.wait_recv()
    together(project(0, count - 1, 0))
    together(attend_own(*range(count)))
    got_code[0].wait_recv()
    got_code[2].wait_recv()
    for w in range(count):
        make_mask(0, w, 1)
    got[0][0].wait_send()
    got[count - 1].append(push(
        atm.at[pl.ds(0, SH), east, :], xs.at[0, 1, pl.ds(body, SH)], -1, 1))
    back = {}

    def send_west(w):
        rows = WH if w < count - 1 else WH - SH

        def done(made):
            ys[0, 1, pl.ds(w * WH, WH)] = made
            back[w] = push(
                ys.at[0, 1, pl.ds(w * WH, rows)], xs.at[1, 1, pl.ds(SH + w * WH, rows)], 0, -1)

        return done

    def send_corner():
        back["corner"] = push(
            ys.at[0, 1, pl.ds(body, SH)], xs.at[1, 1, pl.ds(0, SH)], 1, -1)

    def keep_own(w):
        rows = WH if w < count - 1 else WH - SH

        def done(made):
            xs[1, 0, pl.ds(SH + w * WH, rows)] = made[:rows]
            if w == count - 1:
                ys[0, 0, pl.ds(body, SH)] = made[rows:]
                back["lat"] = push(
                    ys.at[0, 0, pl.ds(body, SH)], xs.at[1, 0, pl.ds(0, SH)], 1, 0)

        return done

    def give(w, h):
        def done(made):
            out[pl.ds(w * WH, WH), pl.ds(SW * h, SW), :] = made

        return done

    waiting = []
    for w in range(count):
        for copy in got[w]:
            copy.wait_recv()
        together(project(0, w, 1), *waiting)
        together(attend(w, 1))
        if w == 0:
            for name in ("out", "up", "down"):
                weights[name, 0].wait()
        away, kept = finish(0, w, 1, send_west(w)), finish(0, w, 0, keep_own(w))
        together(attend_rest(w), away)
        waiting = [kept]
    weights["in", 1].wait()
    early = [project(1, w, 0, SH * (w == 0), SH) for w in (0, count - 1)]
    early = early + [project(1, w, 0) for w in range(1, count - 1)]
    together(kept, chain(masks(1), *early))
    for name in ("out", "up", "down"):
        weights[name, 1].wait()
    send_corner()
    together(project(1, count - 1, 0, SH, SH))
    together(attend_own(*range(1, count)))
    back["lat"].wait_recv()
    together(project(1, 0, 0, 0, SH))
    together(attend_own(0))
    waited = set()
    waiting = []
    for w in reversed(range(count)):
        for v in (w - 1, w):
            if v >= 0 and v not in waited:
                waited.add(v)
                back[v].wait_recv()
        if w == 0:
            back["corner"].wait_recv()
        together(project(1, w, 1), *waiting[:1])
        together(chain(attend(w, 1), attend_rest(w)), *waiting[1:])
        waiting = [finish(1, w, 1, give(w, 1)), finish(1, w, 0, give(w, 0))]
    together(*waiting)
    for copy in sent:
        if copy is not got[0][0]:
            copy.wait_send()


def solution(mesh):
    names = tuple(mesh.axis_names)
    sizes = dict(mesh.shape)

    def on_device(atm, band, valid, gains, w_in, w_out, w_up, w_down):
        height, breadth, width = atm.shape
        hidden = w_up.shape[2]
        count = height // WH
        cells = WH * SW
        pairs = width // 128
        chunks = height // SH
        anyspace = pl.BlockSpec(memory_space=pl.ANY)
        vmem = pl.BlockSpec(memory_space=pltpu.VMEM)
        pushes = 2 * count + 7
        return pl.pallas_call(
            functools.partial(kernel, names, sizes),
            out_shape=pltpu.VMEM(atm.shape, BF16),
            in_specs=[anyspace] * 8,
            out_specs=vmem,
            scratch_shapes=[
                pltpu.VMEM((2, 2, height, SW, width), BF16),
                pltpu.VMEM((1, 2, height, SW, width), BF16),
                pltpu.VMEM((2, chunks, 8, SH * SW), jnp.int32),
                pltpu.VMEM((2, chunks, 8, SH * SW), jnp.int32),
                pltpu.VMEM((1, height), jnp.int32),
                pltpu.VMEM((breadth, height), jnp.int32),
                pltpu.VMEM(gains.shape, F32),
                pltpu.VMEM(w_in.shape, BF16),
                pltpu.VMEM(w_out.shape, BF16),
                pltpu.VMEM(w_up.shape, BF16),
                pltpu.VMEM(w_down.shape, BF16),
                pltpu.VMEM((count, 2 * pairs, 2 * cells, 128), BF16),
                pltpu.VMEM((count, 2 * pairs, 2 * cells, 128), BF16),
                pltpu.VMEM((count, 2 * pairs, 80, 2 * cells), BF16),
                pltpu.VMEM((count, 2, 2 * cells, 128), F32),
                pltpu.VMEM((count, 2 * pairs, 80, cells), F32),
                pltpu.VMEM((2 * count, width, cells), F32),
                pltpu.SemaphoreType.DMA((pushes,)),
                pltpu.SemaphoreType.DMA((pushes,)),
                pltpu.SemaphoreType.DMA((12,)),
            ],
            compiler_params=pltpu.CompilerParams(
                collective_id=0, has_side_effects=True, vmem_limit_bytes=56 * 1024 * 1024
            ),
        )(atm, band[None, :], valid.T, gains, w_in, w_out, w_up, w_down)

    rows = P(("groups", "lat"), "lon", None)
    return jax.shard_map(
        on_device,
        mesh=mesh,
        in_specs=(rows, P(("groups", "lat")), P(("groups", "lat"), "lon"), P(), P(), P(), P(), P()),
        out_specs=rows,
        check_vma=False,
    )
```

time: 40.6 us -> 37.9 us (0.933)
  Pallas kernels: 39.5 us -> 36.7 us
    pallas_call x1, Pallas kernels: 39.5 us -> 36.7 us  [on_device(): pl.pallas_call(functools.partial(kernel, names, sizes), out_shape=pltpu.V...]
where the time goes in v2:
time: 37.9 us; the launch traced here: 37.7 us
  Pallas kernels  36.7 us (97%)
  local copies, waits for them, and re-layouts  0.97 us (3%)
    pallas_call x1, Pallas kernels, on_device(): pl.pallas_call(functools.partial(kernel, names, sizes), out_shape=pltpu.V...  36.7 us
    unnamed x1, local copies, waits for them, and re-layouts  0.97 us

profile of v2, /device:TPU:0, one launch (start us, length us, event | category | flops | bytes accessed | tf_op | source)
XLA Modules:
  0.0 37.7 jit_solution(14773798638208476231)
XLA Ops:
  0.0 36.7 %shard_map.82 = bf16[64,16,512]{2,1,0:T(8,128)(2,1)S(1)} custom-call(bf16[64,16,512]{2,1,0:T(8,128)(2,1)} %atm.1, s32[1,64]{1,0:T(1,128)} %bitcast.3, s32[16,64]{1,0:T(8,128)} %bitcast.2, f32[2,2,512]{2,1,0:T(2,128)} %gains_in.1, bf16[2,512,1536]{2,1,0:T(8,128)(2,1)} %w_in.1, bf16[2,512,512]{2,1,0:T(8,128)(2,1)} %w_out.1, bf16[2,512,1024]{2,1,0:T(8,128)(2,1)} %w_up.1, ...), custom_call_target="tpu_custom_call" | custom-call | tf_op jit(solution)/shard_map/pallas_call | solution.py:424
  36.7 1.0 %copy.10 = bf16[64,16,512]{2,1,0:T(8,128)(2,1)} copy(bf16[64,16,512]{2,1,0:T(8,128)(2,1)S(1)} %shard_map.82) | data formatting | bytes 2097152

commit v3 on v2

--- a/solution.py
+++ b/solution.py
@@ -18,7 +18,7 @@
 BF16 = jnp.bfloat16
 BAND_BITS = 7
 FAR = -1e30
-DEPTH = 3
+UNITS = 8
 
 
 def norm(wide, gains):
@@ -75,6 +75,29 @@
             ("in", w_in, win), ("out", w_out, wout), ("up", w_up, wup), ("down", w_down, wdown),
         ):
             weights[name, layer] = load(src.at[layer], dst.at[layer])
+
+    pl.semaphore_wait(barrier, len(sources))
+
+    sent = []
+
+    def push(src, dst, lat, lon):
+        copy = pltpu.make_async_remote_copy(
+            src_ref=src, dst_ref=dst, send_sem=send.at[len(sent)], recv_sem=recv.at[len(sent)],
+            device_id=device(lat, lon), device_id_type=MESH,
+        )
+        copy.start()
+        sent.append(copy)
+        return copy
+
+    def push_piece(w, first, rows):
+        return push(
+            atm.at[pl.ds(SH + w * WH + first, rows), east, :],
+            xs.at[0, 1, pl.ds(w * WH + first, rows)], 0, 1)
+
+    got = [[] for _ in range(count)]
+    whole = [WH if w < count - 1 else WH - SH for w in range(count)]
+    got[0].append(push_piece(0, 0, SH // 2))
+    got_lat = push(atm.at[pl.ds(0, SH), west, :], xs.at[0, 0, pl.ds(body, SH)], -1, 0)
 
     for copy in small:
         copy.wait()
@@ -92,30 +115,16 @@
             rows = jnp.sum(rows, 0, keepdims=True).astype(jnp.int32)
             code[h, chunk] = jnp.broadcast_to(rows, (8, SH * SW))
 
-    pl.semaphore_wait(barrier, len(sources))
-
-    sent = []
-
-    def push(src, dst, lat, lon):
-        copy = pltpu.make_async_remote_copy(
-            src_ref=src, dst_ref=dst, send_sem=send.at[len(sent)], recv_sem=recv.at[len(sent)],
-            device_id=device(lat, lon), device_id_type=MESH,
-        )
-        copy.start()
-        sent.append(copy)
-        return copy
-
     got_code = [
         push(code.at[1, pl.ds(1, last)], cs.at[1, pl.ds(0, last)], 0, 1),
         push(code.at[0, pl.ds(0, 1)], cs.at[0, pl.ds(last, 1)], -1, 0),
         push(code.at[1, pl.ds(0, 1)], cs.at[1, pl.ds(last, 1)], -1, 1),
     ]
-    got = []
-    for w in range(count):
-        rows = WH if w < count - 1 else WH - SH
-        got.append([push(
-            atm.at[pl.ds(SH + w * WH, rows), east, :], xs.at[0, 1, pl.ds(w * WH, rows)], 0, 1)])
-    got_lat = push(atm.at[pl.ds(0, SH), west, :], xs.at[0, 0, pl.ds(body, SH)], -1, 0)
+    got[0].append(push_piece(0, SH // 2, SH // 2))
+    if whole[0] > SH:
+        got[0].append(push_piece(0, SH, SH))
+    for w in range(1, count):
+        got[w].append(push_piece(w, 0, whole[w]))
 
     vs[:, :, pl.ds(64, 16), :] = jnp.ones(vs.shape[:2] + (16, vs.shape[3]), BF16)
     low = lax.broadcasted_iota(jnp.int32, (cells, 128), 1) < 64
@@ -199,57 +208,52 @@
         return jnp.dot(
             vs[w, j, :, pl.ds(cells * c, cells)], raw, preferred_element_type=F32)
 
-    def attend(w, h):
-        flight = []
-
-        def close():
-            j, made, tops = flight.pop(0)
+    def pipeline(items):
+        def steps():
+            flight = []
+            for size, begin, end in items:
+                flight.append((size, end, begin()))
+                while sum(one[0] for one in flight) > UNITS:
+                    _, close, state = flight.pop(0)
+                    close(*state)
+                yield
+            for _, close, state in flight:
+                close(*state)
+                yield
+
+        return len(items) + UNITS // items[-1][0], steps()
+
+    def whole_item(w, j):
+        def begin():
+            made = [score(w, j, 1, c) for c in range(2)]
+            return made, [jnp.max(one, 0, keepdims=True) for one in made]
+
+        def end(made, tops):
             top = jnp.maximum(tops[0], tops[1])
             total = weigh(w, j, 0, made[0], top) + weigh(w, j, 1, made[1], top)
-            ctx[2 * w + h, pl.ds(64 * j, 64), :] = total[:64] / total[64:65]
-
-        def steps():
-            for j in range(heads):
-                made = [score(w, j, h, c) for c in range(2)]
-                flight.append((j, made, [jnp.max(one, 0, keepdims=True) for one in made]))
-                if len(flight) > DEPTH:
-                    close()
-                yield
-            while flight:
-                close()
-                yield
-
-        return heads + DEPTH, steps()
-
-    def attend_half(units, c, close):
-        flight = []
-
-        def end():
-            w, j, made, top = flight.pop(0)
-            close(w, j, weigh(w, j, c, made, top), top)
-
-        def steps():
-            for w, j in units:
-                made = score(w, j, 0, c)
-                flight.append((w, j, made, jnp.max(made, 0, keepdims=True)))
-                if len(flight) > 2 * DEPTH:
-                    end()
-                yield
-            while flight:
-                end()
-                yield
-
-        return len(units) + 2 * DEPTH, steps()
-
-    def attend_own(*windows):
-        def close(w, j, part, top):
+            ctx[2 * w + 1, pl.ds(64 * j, 64), :] = total[:64] / total[64:65]
+
+        return 2, begin, end
+
+    def half_item(w, j, c, close):
+        def begin():
+            made = score(w, j, 0, c)
+            return made, jnp.max(made, 0, keepdims=True)
+
+        def end(made, top):
+            close(weigh(w, j, c, made, top), top)
+
+        return 1, begin, end
+
+    def own_item(w, j):
+        def close(part, top):
             acc[w, j, pl.ds(0, 72), :] = part[:72]
             acc[w, j, pl.ds(72, 8), :] = jnp.broadcast_to(top, (8, cells))
 
-        return attend_half([(w, j) for w in windows for j in range(heads)], 0, close)
-
-    def attend_rest(w):
-        def close(w, j, part, top):
+        return half_item(w, j, 0, close)
+
+    def rest_item(w, j):
+        def close(part, top):
             first = acc[w, j, pl.ds(0, 64), :]
             first_sum = acc[w, j, pl.ds(64, 8), :][0:1]
             first_top = acc[w, j, pl.ds(72, 8), :][0:1]
@@ -259,7 +263,20 @@
             ctx[2 * w, pl.ds(64 * j, 64), :] = (
                 first * (mine * share) + part[:64] * (theirs * share))
 
-        return attend_half([(w, j) for j in range(heads)], 1, close)
+        return half_item(w, j, 1, close)
+
+    def attend(w):
+        return pipeline([whole_item(w, j) for j in range(heads)])
+
+    def attend_own(*windows):
+        return pipeline([own_item(w, j) for w in windows for j in range(heads)])
+
+    def attend_rest(w):
+        return pipeline([rest_item(w, j) for j in range(heads)])
+
+    def attend_both(w):
+        return pipeline(
+            [whole_item(w, j) for j in range(heads)] + [rest_item(w, j) for j in range(heads)])
 
     def finish(layer, w, h, done):
         step = 256
@@ -304,7 +321,7 @@
             for _, work in works:
                 yield from work
 
-        return sum(size for size, _ in works), steps()
+        return max(1, sum(size for size, _ in works)), steps()
 
     def together(*works):
         left = [[0, size, work] for size, work in works]
@@ -324,11 +341,15 @@
     got_lat.wait_recv()
     together(project(0, count - 1, 0))
     together(attend_own(*range(count)))
+    for name in ("out", "up", "down"):
+        weights[name, 0].wait()
     got_code[0].wait_recv()
     got_code[2].wait_recv()
     for w in range(count):
         make_mask(0, w, 1)
-    got[0][0].wait_send()
+    gone = list(got[0])
+    for copy in gone:
+        copy.wait_send()
     got[count - 1].append(push(
         atm.at[pl.ds(0, SH), east, :], xs.at[0, 1, pl.ds(body, SH)], -1, 1))
     back = {}
@@ -367,43 +388,48 @@
 
     waiting = []
     for w in range(count):
-        for copy in got[w]:
+        for copy in got[w][:-1]:
             copy.wait_recv()
-        together(project(0, w, 1), *waiting)
-        together(attend(w, 1))
-        if w == 0:
-            for name in ("out", "up", "down"):
-                weights[name, 0].wait()
+        if len(got[w]) > 1:
+            together(project(0, w, 1, 0, SH), *waiting)
+            got[w][-1].wait_recv()
+            together(project(0, w, 1, SH, SH))
+        else:
+            got[w][0].wait_recv()
+            together(project(0, w, 1), *waiting)
+        if w == count - 1:
+            for name in ("in", "out", "up", "down"):
+                weights[name, 1].wait()
+        together(attend(w))
         away, kept = finish(0, w, 1, send_west(w)), finish(0, w, 0, keep_own(w))
         together(attend_rest(w), away)
         waiting = [kept]
-    weights["in", 1].wait()
     early = [project(1, w, 0, SH * (w == 0), SH) for w in (0, count - 1)]
     early = early + [project(1, w, 0) for w in range(1, count - 1)]
     together(kept, chain(masks(1), *early))
-    for name in ("out", "up", "down"):
-        weights[name, 1].wait()
-    send_corner()
     together(project(1, count - 1, 0, SH, SH))
     together(attend_own(*range(1, count)))
+    send_corner()
     back["lat"].wait_recv()
-    together(project(1, 0, 0, 0, SH))
-    together(attend_own(0))
-    waited = set()
+    for w in range(count - 1):
+        back[w].wait_recv()
+    together(
+        chain(project(1, 0, 0, 0, SH), attend_own(0)),
+        chain(*(project(1, w, 1, 0, SH) for w in reversed(range(1, count)))))
+    back[count - 1].wait_recv()
+    together(project(1, count - 1, 1, SH, SH))
     waiting = []
     for w in reversed(range(count)):
-        for v in (w - 1, w):
-            if v >= 0 and v not in waited:
-                waited.add(v)
-                back[v].wait_recv()
         if w == 0:
             back["corner"].wait_recv()
-        together(project(1, w, 1), *waiting[:1])
-        together(chain(attend(w, 1), attend_rest(w)), *waiting[1:])
+            together(project(1, w, 1, 0, SH), *waiting[:1])
+            waiting = waiting[1:]
+        ahead = [project(1, w - 1, 1, SH, SH)] if w > 0 else []
+        together(attend_both(w), *ahead, *waiting)
         waiting = [finish(1, w, 1, give(w, 1)), finish(1, w, 0, give(w, 0))]
     together(*waiting)
     for copy in sent:
-        if copy is not got[0][0]:
+        if all(copy is not one for one in gone):
             copy.wait_send()
 
 
@@ -420,7 +446,7 @@
         chunks = height // SH
         anyspace = pl.BlockSpec(memory_space=pl.ANY)
         vmem = pl.BlockSpec(memory_space=pltpu.VMEM)
-        pushes = 2 * count + 7
+        pushes = 2 * count + 9
         return pl.pallas_call(
             functools.partial(kernel, names, sizes),
             out_shape=pltpu.VMEM(atm.shape, BF16),

time: 37.9 us -> 37.6 us (level)
  no operation moved by 1% of the time
where the time goes in v3:
time: 37.6 us; the launch traced here: 37.4 us
  Pallas kernels  36.5 us (97%)
  local copies, waits for them, and re-layouts  0.97 us (3%)
    pallas_call x1, Pallas kernels, on_device(): pl.pallas_call(functools.partial(kernel, names, sizes), out_shape=pltpu.V...  36.5 us
    unnamed x1, local copies, waits for them, and re-layouts  0.97 us

profile of v3, /device:TPU:0, one launch (start us, length us, event | category | flops | bytes accessed | tf_op | source)
XLA Modules:
  0.0 37.4 jit_solution(17924968642519478415)
XLA Ops:
  0.0 36.5 %shard_map.82 = bf16[64,16,512]{2,1,0:T(8,128)(2,1)S(1)} custom-call(bf16[64,16,512]{2,1,0:T(8,128)(2,1)} %atm.1, s32[1,64]{1,0:T(1,128)} %bitcast.3, s32[16,64]{1,0:T(8,128)} %bitcast.2, f32[2,2,512]{2,1,0:T(2,128)} %gains_in.1, bf16[2,512,1536]{2,1,0:T(8,128)(2,1)} %w_in.1, bf16[2,512,512]{2,1,0:T(8,128)(2,1)} %w_out.1, bf16[2,512,1024]{2,1,0:T(8,128)(2,1)} %w_up.1, ...), custom_call_target="tpu_custom_call" | custom-call | tf_op jit(solution)/shard_map/pallas_call | solution.py:450
  36.5 1.0 %copy.10 = bf16[64,16,512]{2,1,0:T(8,128)(2,1)} copy(bf16[64,16,512]{2,1,0:T(8,128)(2,1)S(1)} %shard_map.82) | data formatting | bytes 2097152

commit v4 on v3

--- a/solution.py
+++ b/solution.py
@@ -18,7 +18,7 @@
 BF16 = jnp.bfloat16
 BAND_BITS = 7
 FAR = -1e30
-UNITS = 8
+UNITS = 6
 
 
 def norm(wide, gains):
@@ -178,7 +178,7 @@
                 made = jnp.dot(
                     normed, win[layer, :, pl.ds(part * width, width)], preferred_element_type=F32)
                 if part == 2:
-                    turned = made.T.astype(BF16)
+                    turned = made.astype(BF16).T
                     for head in range(2 * pairs):
                         vs[w, head, pl.ds(0, 64), where] = turned[64 * head:64 * head + 64]
                     yield
@@ -231,7 +231,7 @@
         def end(made, tops):
             top = jnp.maximum(tops[0], tops[1])
             total = weigh(w, j, 0, made[0], top) + weigh(w, j, 1, made[1], top)
-            ctx[2 * w + 1, pl.ds(64 * j, 64), :] = total[:64] / total[64:65]
+            ctx[2 * w + 1, pl.ds(64 * j, 64), :] = (total[:64] / total[64:65]).astype(BF16)
 
         return 2, begin, end
 
@@ -261,7 +261,7 @@
             mine, theirs = jnp.exp2(first_top - joint), jnp.exp2(top - joint)
             share = 1.0 / (first_sum * mine + part[64:65] * theirs)
             ctx[2 * w, pl.ds(64 * j, 64), :] = (
-                first * (mine * share) + part[:64] * (theirs * share))
+                first * (mine * share) + part[:64] * (theirs * share)).astype(BF16)
 
         return half_item(w, j, 1, close)
 
@@ -282,7 +282,7 @@
         step = 256
 
         def steps():
-            turned = ctx[2 * w + h].T.astype(BF16)
+            turned = ctx[2 * w + h].T
             own_field = field(layer, w, h)
             parts = []
             for n in range(0, width, step):
@@ -422,10 +422,9 @@
     for w in reversed(range(count)):
         if w == 0:
             back["corner"].wait_recv()
-            together(project(1, w, 1, 0, SH), *waiting[:1])
-            waiting = waiting[1:]
+        first = [project(1, w, 1, 0, SH)] if w == 0 else []
         ahead = [project(1, w - 1, 1, SH, SH)] if w > 0 else []
-        together(attend_both(w), *ahead, *waiting)
+        together(chain(*first, attend_both(w)), *ahead, *waiting)
         waiting = [finish(1, w, 1, give(w, 1)), finish(1, w, 0, give(w, 0))]
     together(*waiting)
     for copy in sent:
@@ -469,7 +468,7 @@
                 pltpu.VMEM((count, 2 * pairs, 80, 2 * cells), BF16),
                 pltpu.VMEM((count, 2, 2 * cells, 128), F32),
                 pltpu.VMEM((count, 2 * pairs, 80, cells), F32),
-                pltpu.VMEM((2 * count, width, cells), F32),
+                pltpu.VMEM((2 * count, width, cells), BF16),
                 pltpu.SemaphoreType.DMA((pushes,)),
                 pltpu.SemaphoreType.DMA((pushes,)),
                 pltpu.SemaphoreType.DMA((12,)),

time: 37.6 us -> 37.4 us (level)
  no operation moved by 1% of the time
where the time goes in v4:
time: 37.4 us; the launch traced here: 37.2 us
  Pallas kernels  36.2 us (97%)
  local copies, waits for them, and re-layouts  0.97 us (3%)
    pallas_call x1, Pallas kernels, on_device(): pl.pallas_call(functools.partial(kernel, names, sizes), out_shape=pltpu.V...  36.2 us
    unnamed x1, local copies, waits for them, and re-layouts  0.97 us

profile of v4, /device:TPU:0, one launch (start us, length us, event | category | flops | bytes accessed | tf_op | source)
XLA Modules:
  0.0 37.2 jit_solution(9621340010385816523)
XLA Ops:
  0.0 36.2 %shard_map.82 = bf16[64,16,512]{2,1,0:T(8,128)(2,1)S(1)} custom-call(bf16[64,16,512]{2,1,0:T(8,128)(2,1)} %atm.1, s32[1,64]{1,0:T(1,128)} %bitcast.3, s32[16,64]{1,0:T(8,128)} %bitcast.2, f32[2,2,512]{2,1,0:T(2,128)} %gains_in.1, bf16[2,512,1536]{2,1,0:T(8,128)(2,1)} %w_in.1, bf16[2,512,512]{2,1,0:T(8,128)(2,1)} %w_out.1, bf16[2,512,1024]{2,1,0:T(8,128)(2,1)} %w_up.1, ...), custom_call_target="tpu_custom_call" | custom-call | tf_op jit(solution)/shard_map/pallas_call | solution.py:449
  36.2 1.0 %copy.10 = bf16[64,16,512]{2,1,0:T(8,128)(2,1)} copy(bf16[64,16,512]{2,1,0:T(8,128)(2,1)S(1)} %shard_map.82) | data formatting | bytes 2097152
